TPU v7x, 32 devices: a whole 2x2x4 slice. The times are simulated.
32 devices in a mesh: dp: 4 (over z), shard: 8 (over y, x, core).
Axes of the slice: x: 2, y: 2, z: 4, core: 2. Of those that a mesh axis runs over, the one named last changes fastest.
Arguments:
- hidden: bfloat16 [192, 256, 1024], P(('dp', 'shard')), may hold values from -40 to 40, as said below
- lengths: int32 [192], replicated, may hold values from 16 to 256
- dealing: int32 [192], replicated, may hold values from 0 to 191, each once
- candidates: int32 [192, 64], P(('dp', 'shard')), may hold values from 0 to 131071
- index_rows: bfloat16 [131072, 1024], P(('dp', 'shard')), may hold values from -6 to 6
- qkv_weight: bfloat16 [1024, 3072], replicated, may hold values from -0.1875 to 0.1875
- qkv_bias: float32 [3072], replicated, may hold values from -3 to 3
- out_weight: bfloat16 [1024, 1024], replicated, may hold values from -0.1875 to 0.1875
- out_bias: float32 [1024], replicated, may hold values from -3 to 3
- norm_gain: float32 [1024], replicated, may hold values from 0.25 to 1.75
- norm_shift: float32 [1024], replicated, may hold values from -3 to 3
Outputs:
- scores: float32 [192, 64], P(('dp', 'shard'))
Inputs may be any that keep to these rules, and one draw needn't show every extreme that they name: dealing names every text once. `hidden`: token states of order one, some much larger.
All inputs are finite; a program needn't handle non-finite values.
Results may differ from a plain program's by a relative error of at most 0.0044.
Values may be sent and summed in bfloat16 or wider, within the bound.
A program may use at most 128 MiB of HBM per device.

v0:
```python
import jax
import jax.numpy as jnp
from jax import lax
from jax.sharding import PartitionSpec as P

HEADS = 16
HEAD = 64


def attend(pair):
    text_block, text_lens = pair
    block_count, seq_len, triple = text_block.shape
    model_width = triple // 3
    q_part = text_block[..., :model_width].reshape(block_count, seq_len, HEADS, HEAD)
    k_part = text_block[..., model_width : 2 * model_width].reshape(
        block_count, seq_len, HEADS, HEAD
    )
    v_part = text_block[..., 2 * model_width :].reshape(block_count, seq_len, HEADS, HEAD)
    logits = jnp.einsum("bqhd,bkhd->bhqk", q_part, k_part, preferred_element_type=jnp.float32) * (
        1.0 / HEAD**0.5
    )
    positions = jnp.arange(seq_len, dtype=jnp.int32)
    key_valid = positions[None, :] < text_lens[:, None]
    logits = jnp.where(key_valid[:, None, None, :], logits, -1e30)
    peak = jnp.max(logits, axis=-1, keepdims=True)
    weights = jnp.exp(logits - peak)
    probs = (weights / jnp.sum(weights, axis=-1, keepdims=True)).astype(jnp.bfloat16)
    context = jnp.einsum("bhqk,bkhd->bqhd", probs, v_part, preferred_element_type=jnp.float32)
    return context.reshape(block_count, seq_len, model_width).astype(jnp.bfloat16)


def shards(
    hidden,
    lengths,
    dealing,
    candidates,
    index_rows,
    qkv_weight,
    qkv_bias,
    out_weight,
    out_bias,
    norm_gain,
    norm_shift,
):
    text_dev, seq_len, model_width = hidden.shape
    device_count = lax.axis_size(("dp", "shard"))
    my_rank = lax.axis_index(("dp", "shard"))
    text_total = text_dev * device_count
    my_texts = lax.dynamic_slice_in_dim(dealing, my_rank * text_dev, text_dev)
    my_lens = lengths[my_texts]
    flat_states = hidden.reshape(text_dev * seq_len, model_width)
    qkv = (jnp.dot(flat_states, qkv_weight, preferred_element_type=jnp.float32) + qkv_bias).astype(
        jnp.bfloat16
    )
    qkv_blocks = qkv.reshape(text_dev // 2, 2, seq_len, 3 * model_width)
    len_blocks = my_lens.reshape(text_dev // 2, 2)
    context = lax.map(attend, (qkv_blocks, len_blocks)).reshape(text_dev * seq_len, model_width)
    resid = (
        flat_states.astype(jnp.float32)
        + jnp.dot(context, out_weight, preferred_element_type=jnp.float32)
        + out_bias
    )
    centre = jnp.mean(resid, axis=-1, keepdims=True)
    spread = jnp.mean((resid - centre) ** 2, axis=-1, keepdims=True)
    normed = (resid - centre) * lax.rsqrt(spread + 1e-05) * norm_gain + norm_shift
    normed = normed.reshape(text_dev, seq_len, model_width)
    positions = jnp.arange(seq_len, dtype=jnp.int32)
    token_valid = positions[None, :] < my_lens[:, None]
    pooled = (
        jnp.sum(jnp.where(token_valid[:, :, None], normed, 0.0), axis=1)
        / my_lens.astype(jnp.float32)[:, None]
    )
    queries = (pooled * lax.rsqrt(jnp.sum(pooled * pooled, axis=-1, keepdims=True) + 1e-06)).astype(
        jnp.bfloat16
    )
    all_cands = lax.all_gather(candidates, ("dp", "shard"), axis=0, tiled=True)
    rows_here = index_rows.shape[0]
    row_start = my_rank * rows_here
    slot_local = all_cands[dealing] - row_start
    cand_total = slot_local.shape[1]
    row_iota = jnp.arange(rows_here, dtype=jnp.int32)
    segment = lax.all_gather(queries, ("dp", "shard"), axis=0, tiled=True)
    count_rows = segment.shape[0]
    block_scores = lax.dot_general(
        segment, index_rows, (((1,), (1,)), ((), ())), preferred_element_type=jnp.float32
    )
    column_groups = jnp.transpose(slot_local.reshape(count_rows, cand_total // 4, 4), (1, 0, 2))

    def pick_group(group):
        matches = group[:, :, None] == row_iota[None, None, :]
        return jnp.sum(jnp.where(matches, block_scores[:, None, :], 0.0), axis=-1)

    picked = lax.map(pick_group, column_groups)
    slot_terms = jnp.transpose(picked, (1, 0, 2)).reshape(count_rows, cand_total)
    cand_count = slot_terms.shape[1]
    mine = lax.psum_scatter(slot_terms, ("dp", "shard"), scatter_dimension=0, tiled=True)
    text_slots = jnp.arange(text_total, dtype=jnp.int32)
    outgoing = jnp.zeros((text_total, cand_count), jnp.float32)
    for slot in range(text_dev):
        outgoing = outgoing + jnp.where(
            (text_slots == my_texts[slot])[:, None], mine[slot][None, :], 0.0
        )
    received = lax.all_to_all(outgoing, ("dp", "shard"), split_axis=0, concat_axis=0, tiled=True)
    result = jnp.sum(received.reshape(device_count, text_dev, cand_count), axis=0)
    return result


def solution(mesh):
    in_specs = (
        P(("dp", "shard"), None, None),
        P(),
        P(),
        P(("dp", "shard"), None),
        P(("dp", "shard"), None),
        P(),
        P(),
        P(),
        P(),
        P(),
        P(),
    )
    out_specs = P(("dp", "shard"), None)
    return jax.shard_map(shards, mesh=mesh, in_specs=in_specs, out_specs=out_specs, check_vma=False)
```

profile of v0, /device:TPU:0, one launch (start us, length us, event | category | flops | bytes accessed | tf_op | source)
XLA Modules:
  0.0 319.7 jit_solution(14814296404890690616)
XLA Ops:
  0.9 1.3 gather_fusion.1
  3.1 15.3 %add_convert_fusion = bf16[1536,3072]{1,0:T(8,128)(2,1)} fusion(bf16[1536,1024]{1,0:T(8,128)(2,1)} %bitcast.87, bf16[1024,3072]{1,0:T(8,128)(2,1)} %param.20, f32[3072]{0:T(1024)} %param.21), kind=kOutput, calls=%fused_computation.25 | convolution fusion | flops 9673113600 | bytes 18886656 | tf_op jit(solution)/shard_map/dot_general | solution.py:52
  18.4 83.4 %while.21 = (s32[]{:T(128)}, bf16[3,2,256,1024]{3,2,1,0:T(8,128)(2,1)}, bf16[3,2,256,3072]{3,2,1,0:T(8,128)(2,1)}, s32[3,2]{1,0:T(4,128)S(1)}, s32[]{:T(128)}) while((s32[]{:T(128)}, bf16[3,2,256,1024]{3,2,1,0:T(8,128)(2,1)}, bf16[3,2,256,3072]{3,2,1,0:T(8,128)(2,1)}, s32[3,2]{1,0:T(4,128)S(1)}, s32[]{:T(128)}) %tuple.69), condition=%wide.region_3.4_spmd, body=%wide.region_0.3_spmd.sunk | while | flops 549978880 | bytes 44107356 | solution.py:57
  18.4 3.8 %constant_dynamic-slice_fusion.4 = bf16[1,2,256,3072]{3,2,1,0:T(8,128)(2,1)} fusion(bf16[3,2,256,3072]{3,2,1,0:T(8,128)(2,1)} %get-tuple-element.209, s32[]{:T(128)} %get-tuple-element.202), kind=kLoop, calls=%fused_computation.17.clone.1 | loop fusion | bytes 6291460 | tf_op jit(solution)/shard_map/while/body/jit(dynamic_index_in_dim)/dynamic_slice | solution.py:57
  22.2 4.6 %copy.58 = bf16[1,2,256,3072]{2,3,1,0:T(8,128)(2,1)} copy(bf16[1,2,256,3072]{3,2,1,0:T(8,128)(2,1)} %constant_dynamic-slice_fusion.4) | data formatting | bytes 6291456 | tf_op jit(solution)/shard_map/while/body/jit(dynamic_index_in_dim)/dynamic_slice | solution.py:57
  26.8 3.4 %fusion.47 = (bf16[2,256,1024]{1,2,0:T(8,128)(2,1)}, bf16[2,256,1024]{1,2,0:T(8,128)(2,1)}, bf16[2,256,1024]{1,2,0:T(8,128)(2,1)S(1)}) fusion(bf16[2,256,3072]{1,2,0:T(8,128)(2,1)} %bitcast.77), kind=kLoop, calls=%fused_computation.58.clone.1 | loop fusion | bytes 6291456 | tf_op jit(solution)/shard_map/while/body/eval_jaxpr/slice | solution.py:15
  30.3 8.1 %fusion.49 = (f32[2,16,256]{2,1,0:T(8,128)S(1)}, f32[2,16,256,256]{2,3,1,0:T(8,128)}) fusion(pred[2,256]{1,0:T(4,128)(4,1)S(1)} %iota_compare_fusion.4, bf16[2,256,16,64]{1,3,2,0:T(8,128)(2,1)} %bitcast.82, bf16[2,256,16,64]{1,3,2,0:T(8,128)(2,1)} %bitcast.81), kind=kOutput, calls=%fused_computation.59.clone.1 | convolution fusion | flops 276824320 | bytes 10519040 | tf_op jit(solution)/shard_map/while/body/eval_jaxpr/sub | solution.py:26
  38.5 5.2 %fusion.50 = bf16[2,16,64,256]{3,2,1,0:T(8,128)(2,1)} fusion(bf16[2,256,16,64]{1,3,2,0:T(8,128)(2,1)S(1)} %bitcast.80, f32[2,16,256,256]{2,3,1,0:T(8,128)} %get-tuple-element.191, f32[2,16,256]{2,1,0:T(8,128)S(1)} %get-tuple-element.192), kind=kOutput, calls=%fused_computation.12.clone.1 | convolution fusion | flops 273154048 | bytes 10518528 | tf_op jit(solution)/shard_map/while/body/eval_jaxpr/bhqk,bkhd->bqhd/dot_general | solution.py:28
  43.7 1.5 copy.59
  46.3 3.8 %constant_dynamic-slice_fusion.4 = bf16[1,2,256,3072]{3,2,1,0:T(8,128)(2,1)} fusion(bf16[3,2,256,3072]{3,2,1,0:T(8,128)(2,1)} %get-tuple-element.209, s32[]{:T(128)} %get-tuple-element.202), kind=kLoop, calls=%fused_computation.17.clone.1 | loop fusion | bytes 6291460 | tf_op jit(solution)/shard_map/while/body/jit(dynamic_index_in_dim)/dynamic_slice | solution.py:57
  50.0 4.6 %copy.58 = bf16[1,2,256,3072]{2,3,1,0:T(8,128)(2,1)} copy(bf16[1,2,256,3072]{3,2,1,0:T(8,128)(2,1)} %constant_dynamic-slice_fusion.4) | data formatting | bytes 6291456 | tf_op jit(solution)/shard_map/while/body/jit(dynamic_index_in_dim)/dynamic_slice | solution.py:57
  54.7 3.4 %fusion.47 = (bf16[2,256,1024]{1,2,0:T(8,128)(2,1)}, bf16[2,256,1024]{1,2,0:T(8,128)(2,1)}, bf16[2,256,1024]{1,2,0:T(8,128)(2,1)S(1)}) fusion(bf16[2,256,3072]{1,2,0:T(8,128)(2,1)} %bitcast.77), kind=kLoop, calls=%fused_computation.58.clone.1 | loop fusion | bytes 6291456 | tf_op jit(solution)/shard_map/while/body/eval_jaxpr/slice | solution.py:15
  58.1 8.1 %fusion.49 = (f32[2,16,256]{2,1,0:T(8,128)S(1)}, f32[2,16,256,256]{2,3,1,0:T(8,128)}) fusion(pred[2,256]{1,0:T(4,128)(4,1)S(1)} %iota_compare_fusion.4, bf16[2,256,16,64]{1,3,2,0:T(8,128)(2,1)} %bitcast.82, bf16[2,256,16,64]{1,3,2,0:T(8,128)(2,1)} %bitcast.81), kind=kOutput, calls=%fused_computation.59.clone.1 | convolution fusion | flops 276824320 | bytes 10519040 | tf_op jit(solution)/shard_map/while/body/eval_jaxpr/sub | solution.py:26
  66.3 5.2 %fusion.50 = bf16[2,16,64,256]{3,2,1,0:T(8,128)(2,1)} fusion(bf16[2,256,16,64]{1,3,2,0:T(8,128)(2,1)S(1)} %bitcast.80, f32[2,16,256,256]{2,3,1,0:T(8,128)} %get-tuple-element.191, f32[2,16,256]{2,1,0:T(8,128)S(1)} %get-tuple-element.192), kind=kOutput, calls=%fused_computation.12.clone.1 | convolution fusion | flops 273154048 | bytes 10518528 | tf_op jit(solution)/shard_map/while/body/eval_jaxpr/bhqk,bkhd->bqhd/dot_general | solution.py:28
  71.5 1.5 copy.59
  74.1 3.8 %constant_dynamic-slice_fusion.4 = bf16[1,2,256,3072]{3,2,1,0:T(8,128)(2,1)} fusion(bf16[3,2,256,3072]{3,2,1,0:T(8,128)(2,1)} %get-tuple-element.209, s32[]{:T(128)} %get-tuple-element.202), kind=kLoop, calls=%fused_computation.17.clone.1 | loop fusion | bytes 6291460 | tf_op jit(solution)/shard_map/while/body/jit(dynamic_index_in_dim)/dynamic_slice | solution.py:57
  77.8 4.6 %copy.58 = bf16[1,2,256,3072]{2,3,1,0:T(8,128)(2,1)} copy(bf16[1,2,256,3072]{3,2,1,0:T(8,128)(2,1)} %constant_dynamic-slice_fusion.4) | data formatting | bytes 6291456 | tf_op jit(solution)/shard_map/while/body/jit(dynamic_index_in_dim)/dynamic_slice | solution.py:57
  82.5 3.4 %fusion.47 = (bf16[2,256,1024]{1,2,0:T(8,128)(2,1)}, bf16[2,256,1024]{1,2,0:T(8,128)(2,1)}, bf16[2,256,1024]{1,2,0:T(8,128)(2,1)S(1)}) fusion(bf16[2,256,3072]{1,2,0:T(8,128)(2,1)} %bitcast.77), kind=kLoop, calls=%fused_computation.58.clone.1 | loop fusion | bytes 6291456 | tf_op jit(solution)/shard_map/while/body/eval_jaxpr/slice | solution.py:15
  85.9 8.1 %fusion.49 = (f32[2,16,256]{2,1,0:T(8,128)S(1)}, f32[2,16,256,256]{2,3,1,0:T(8,128)}) fusion(pred[2,256]{1,0:T(4,128)(4,1)S(1)} %iota_compare_fusion.4, bf16[2,256,16,64]{1,3,2,0:T(8,128)(2,1)} %bitcast.82, bf16[2,256,16,64]{1,3,2,0:T(8,128)(2,1)} %bitcast.81), kind=kOutput, calls=%fused_computation.59.clone.1 | convolution fusion | flops 276824320 | bytes 10519040 | tf_op jit(solution)/shard_map/while/body/eval_jaxpr/sub | solution.py:26
  94.1 5.2 %fusion.50 = bf16[2,16,64,256]{3,2,1,0:T(8,128)(2,1)} fusion(bf16[2,256,16,64]{1,3,2,0:T(8,128)(2,1)S(1)} %bitcast.80, f32[2,16,256,256]{2,3,1,0:T(8,128)} %get-tuple-element.191, f32[2,16,256]{2,1,0:T(8,128)S(1)} %get-tuple-element.192), kind=kOutput, calls=%fused_computation.12.clone.1 | convolution fusion | flops 273154048 | bytes 10518528 | tf_op jit(solution)/shard_map/while/body/eval_jaxpr/bhqk,bkhd->bqhd/dot_general | solution.py:28
  99.3 1.5 copy.59
  101.9 6.9 %fusion.24 = (f32[1536]{0:T(1024)S(1)}, f32[1536,1024]{1,0:T(8,128)S(1)}) fusion(f32[1024]{0:T(1024)S(1)} %copy-done.4, bf16[1536,1024]{1,0:T(8,128)(2,1)} %bitcast.89, bf16[1024,1024]{1,0:T(8,128)(2,1)S(1)} %copy-done, bf16[1536,1024]{1,0:T(8,128)(2,1)} %bitcast.88), kind=kOutput, calls=%fused_computation.61 | convolution fusion | flops 3227515392 | bytes 14690304 | tf_op jit(solution)/shard_map/dot_general | solution.py:60
  109.6 1.3 multiply_add_fusion
  111.8 44.6 %all-gather.1 = bf16[32,6,1024]{2,1,0:T(8,128)(2,1)S(1)} all-gather(bf16[1,6,1024]{2,1,0:T(8,128)(2,1)S(1)} %fusion.14), channel_id=1, replica_groups=mesh['dp'=4,'shard'=8] {'dp','shard'}, dimensions={0}, use_global_device_ids=true | all-gather | bytes 405504 | tf_op jit(solution)/shard_map/all_gather | solution.py:82
  156.6 37.0 %all-gather = s32[32,6,64]{2,1,0:T(8,128)S(1)} all-gather(s32[1,6,64]{2,1,0:T(8,128)S(1)} %bitcast.86), channel_id=1, replica_groups=mesh['dp'=4,'shard'=8] {'dp','shard'}, dimensions={0}, use_global_device_ids=true | all-gather | bytes 50688 | tf_op jit(solution)/shard_map/all_gather | solution.py:76
  194.5 8.0 %fusion.25 = f32[192,4096]{1,0:T(8,128)} fusion(bf16[192,1024]{1,0:T(8,128)(2,1)S(1)} %reshape.231, bf16[4096,1024]{1,0:T(8,128)(2,1)} %param.19), kind=kOutput, calls=%fused_computation.62 | convolution fusion | flops 1610612736 | bytes 11927552 | tf_op jit(solution)/shard_map/dot_general | solution.py:84
  202.4 59.2 %while.22 = (s32[]{:T(128)}, f32[16,192,4]{1,2,0:T(4,128)S(1)}, s32[16,192,4]{1,2,0:T(4,128)S(1)}, f32[192,4096]{1,0:T(8,128)}, s32[]{:T(128)}) while((s32[]{:T(128)}, f32[16,192,4]{1,2,0:T(4,128)S(1)}, s32[16,192,4]{1,2,0:T(4,128)S(1)}, f32[192,4096]{1,0:T(8,128)}, s32[]{:T(128)}) %tuple.70), condition=%wide.region_10.11_spmd.clone, body=%wide.region_8.10_spmd.clone.sunk | while | flops 9436418 | bytes 3166277 | solution.py:93
  202.4 3.7 %select_reduce_fusion.3 = f32[192,4]{0,1:T(4,128)S(1)} fusion(f32[192,4096]{1,0:T(8,128)} %get-tuple-element.225, s32[192,4]{0,1:T(4,128)S(1)} %dynamic-slice_bitcast_fusion.2), kind=kLoop, calls=%fused_computation.22.clone.1 | loop fusion | flops 9436416 | bytes 3151872 | tf_op jit(solution)/shard_map/while/body/eval_jaxpr/reduce_sum | solution.py:91
  206.1 3.7 %select_reduce_fusion.3 = f32[192,4]{0,1:T(4,128)S(1)} fusion(f32[192,4096]{1,0:T(8,128)} %get-tuple-element.225, s32[192,4]{0,1:T(4,128)S(1)} %dynamic-slice_bitcast_fusion.2), kind=kLoop, calls=%fused_computation.22.clone.1 | loop fusion | flops 9436416 | bytes 3151872 | tf_op jit(solution)/shard_map/while/body/eval_jaxpr/reduce_sum | solution.py:91
  209.8 3.7 %select_reduce_fusion.3 = f32[192,4]{0,1:T(4,128)S(1)} fusion(f32[192,4096]{1,0:T(8,128)} %get-tuple-element.225, s32[192,4]{0,1:T(4,128)S(1)} %dynamic-slice_bitcast_fusion.2), kind=kLoop, calls=%fused_computation.22.clone.1 | loop fusion | flops 9436416 | bytes 3151872 | tf_op jit(solution)/shard_map/while/body/eval_jaxpr/reduce_sum | solution.py:91
  213.5 3.7 %select_reduce_fusion.3 = f32[192,4]{0,1:T(4,128)S(1)} fusion(f32[192,4096]{1,0:T(8,128)} %get-tuple-element.225, s32[192,4]{0,1:T(4,128)S(1)} %dynamic-slice_bitcast_fusion.2), kind=kLoop, calls=%fused_computation.22.clone.1 | loop fusion | flops 9436416 | bytes 3151872 | tf_op jit(solution)/shard_map/while/body/eval_jaxpr/reduce_sum | solution.py:91
  217.2 3.7 %select_reduce_fusion.3 = f32[192,4]{0,1:T(4,128)S(1)} fusion(f32[192,4096]{1,0:T(8,128)} %get-tuple-element.225, s32[192,4]{0,1:T(4,128)S(1)} %dynamic-slice_bitcast_fusion.2), kind=kLoop, calls=%fused_computation.22.clone.1 | loop fusion | flops 9436416 | bytes 3151872 | tf_op jit(solution)/shard_map/while/body/eval_jaxpr/reduce_sum | solution.py:91
  220.9 3.7 %select_reduce_fusion.3 = f32[192,4]{0,1:T(4,128)S(1)} fusion(f32[192,4096]{1,0:T(8,128)} %get-tuple-element.225, s32[192,4]{0,1:T(4,128)S(1)} %dynamic-slice_bitcast_fusion.2), kind=kLoop, calls=%fused_computation.22.clone.1 | loop fusion | flops 9436416 | bytes 3151872 | tf_op jit(solution)/shard_map/while/body/eval_jaxpr/reduce_sum | solution.py:91
  224.7 3.7 %select_reduce_fusion.3 = f32[192,4]{0,1:T(4,128)S(1)} fusion(f32[192,4096]{1,0:T(8,128)} %get-tuple-element.225, s32[192,4]{0,1:T(4,128)S(1)} %dynamic-slice_bitcast_fusion.2), kind=kLoop, calls=%fused_computation.22.clone.1 | loop fusion | flops 9436416 | bytes 3151872 | tf_op jit(solution)/shard_map/while/body/eval_jaxpr/reduce_sum | solution.py:91
  228.4 3.7 %select_reduce_fusion.3 = f32[192,4]{0,1:T(4,128)S(1)} fusion(f32[192,4096]{1,0:T(8,128)} %get-tuple-element.225, s32[192,4]{0,1:T(4,128)S(1)} %dynamic-slice_bitcast_fusion.2), kind=kLoop, calls=%fused_computation.22.clone.1 | loop fusion | flops 9436416 | bytes 3151872 | tf_op jit(solution)/shard_map/while/body/eval_jaxpr/reduce_sum | solution.py:91
  232.1 3.7 %select_reduce_fusion.3 = f32[192,4]{0,1:T(4,128)S(1)} fusion(f32[192,4096]{1,0:T(8,128)} %get-tuple-element.225, s32[192,4]{0,1:T(4,128)S(1)} %dynamic-slice_bitcast_fusion.2), kind=kLoop, calls=%fused_computation.22.clone.1 | loop fusion | flops 9436416 | bytes 3151872 | tf_op jit(solution)/shard_map/while/body/eval_jaxpr/reduce_sum | solution.py:91
  235.8 3.7 %select_reduce_fusion.3 = f32[192,4]{0,1:T(4,128)S(1)} fusion(f32[192,4096]{1,0:T(8,128)} %get-tuple-element.225, s32[192,4]{0,1:T(4,128)S(1)} %dynamic-slice_bitcast_fusion.2), kind=kLoop, calls=%fused_computation.22.clone.1 | loop fusion | flops 9436416 | bytes 3151872 | tf_op jit(solution)/shard_map/while/body/eval_jaxpr/reduce_sum | solution.py:91
  239.5 3.7 %select_reduce_fusion.3 = f32[192,4]{0,1:T(4,128)S(1)} fusion(f32[192,4096]{1,0:T(8,128)} %get-tuple-element.225, s32[192,4]{0,1:T(4,128)S(1)} %dynamic-slice_bitcast_fusion.2), kind=kLoop, calls=%fused_computation.22.clone.1 | loop fusion | flops 9436416 | bytes 3151872 | tf_op jit(solution)/shard_map/while/body/eval_jaxpr/reduce_sum | solution.py:91
  243.2 3.7 %select_reduce_fusion.3 = f32[192,4]{0,1:T(4,128)S(1)} fusion(f32[192,4096]{1,0:T(8,128)} %get-tuple-element.225, s32[192,4]{0,1:T(4,128)S(1)} %dynamic-slice_bitcast_fusion.2), kind=kLoop, calls=%fused_computation.22.clone.1 | loop fusion | flops 9436416 | bytes 3151872 | tf_op jit(solution)/shard_map/while/body/eval_jaxpr/reduce_sum | solution.py:91
  246.9 3.7 %select_reduce_fusion.3 = f32[192,4]{0,1:T(4,128)S(1)} fusion(f32[192,4096]{1,0:T(8,128)} %get-tuple-element.225, s32[192,4]{0,1:T(4,128)S(1)} %dynamic-slice_bitcast_fusion.2), kind=kLoop, calls=%fused_computation.22.clone.1 | loop fusion | flops 9436416 | bytes 3151872 | tf_op jit(solution)/shard_map/while/body/eval_jaxpr/reduce_sum | solution.py:91
  250.6 3.7 %select_reduce_fusion.3 = f32[192,4]{0,1:T(4,128)S(1)} fusion(f32[192,4096]{1,0:T(8,128)} %get-tuple-element.225, s32[192,4]{0,1:T(4,128)S(1)} %dynamic-slice_bitcast_fusion.2), kind=kLoop, calls=%fused_computation.22.clone.1 | loop fusion | flops 9436416 | bytes 3151872 | tf_op jit(solution)/shard_map/while/body/eval_jaxpr/reduce_sum | solution.py:91
  254.3 3.7 %select_reduce_fusion.3 = f32[192,4]{0,1:T(4,128)S(1)} fusion(f32[192,4096]{1,0:T(8,128)} %get-tuple-element.225, s32[192,4]{0,1:T(4,128)S(1)} %dynamic-slice_bitcast_fusion.2), kind=kLoop, calls=%fused_computation.22.clone.1 | loop fusion | flops 9436416 | bytes 3151872 | tf_op jit(solution)/shard_map/while/body/eval_jaxpr/reduce_sum | solution.py:91
  258.0 3.7 %select_reduce_fusion.3 = f32[192,4]{0,1:T(4,128)S(1)} fusion(f32[192,4096]{1,0:T(8,128)} %get-tuple-element.225, s32[192,4]{0,1:T(4,128)S(1)} %dynamic-slice_bitcast_fusion.2), kind=kLoop, calls=%fused_computation.22.clone.1 | loop fusion | flops 9436416 | bytes 3151872 | tf_op jit(solution)/shard_map/while/body/eval_jaxpr/reduce_sum | solution.py:91
  261.8 37.9 %all-reduce = f32[192,64]{1,0:T(8,128)S(1)} all-reduce(f32[192,64]{1,0:T(8,128)S(1)} %copy.49), channel_id=2, replica_groups=mesh['dp'=4,'shard'=8] {'dp','shard'}, use_global_device_ids=true, to_apply=%region_11.12.clone | all-reduce | flops 12288 | bytes 98304
  300.4 1.2 fusion.15
  301.6 1.3 fusion.17
  303.0 1.2 fusion.19
  304.6 13.1 %all_to_all.6 = f32[32,1,384]{2,1,0:T(1,128)S(1)} all-to-all(f32[32,1,384]{2,1,0:T(1,128)S(1)} %reshape.232), channel_id=1, replica_groups=mesh['dp'=4,'shard'=8] {'dp','shard'}, dimensions={0} | all-to-all | bytes 98304 | tf_op jit(solution)/shard_map/all_to_all | solution.py:103
  (84 shorter events, 11.4 us)
Async XLA Ops:
  0.0 101.9 %copy-start = (bf16[1024,1024]{1,0:T(8,128)(2,1)S(1)}, bf16[1024,1024]{1,0:T(8,128)(2,1)}, u32[]{:S(2)}) copy-start(bf16[1024,1024]{1,0:T(8,128)(2,1)} %param.22) | copy-start | bytes 6291460
  18.4 83.4 %copy-start.4 = (f32[1024]{0:T(1024)S(1)}, f32[1024]{0:T(1024)}, u32[]{:S(2)}) copy-start(f32[1024]{0:T(1024)} %param.23) | copy-start | bytes 12292
  108.8 0.8 copy-start.1
  108.8 0.8 copy-start.2
  110.9 45.7 %copy-start.3 = (s32[6,64]{1,0:T(8,128)S(1)}, s32[6,64]{1,0:T(8,128)}, u32[]{:S(2)}) copy-start(s32[6,64]{1,0:T(8,128)} %param.18) | copy-start | bytes 4612
where the time goes:
time: 321 us; the launch traced here: 320 us
  blocking collectives  133 us (41%)
  matrix products  70.3 us (22%)
  other arithmetic  68.9 us (21%)
  local copies, waits for them, and re-layouts  47.3 us (15%)
    reduce_sum x16, other arithmetic, pick_group(): return jnp.sum(jnp.where(matches, block_scores[:, None, :], 0.0), axis=-1)  58.5 us
    all_gather x1, blocking collectives, shards(): segment = lax.all_gather(queries, ('dp', 'shard'), axis=0, tiled=True)  44.6 us
    unnamed x1, blocking collectives  37.9 us
    all_gather x1, blocking collectives, shards(): all_cands = lax.all_gather(candidates, ('dp', 'shard'), axis=0, tiled=True)  37 us
    dynamic_slice x6, local copies, waits for them, and re-layouts, shards(): lax.map(attend, (qkv_blocks, len_blocks))  25.2 us
    sub x3, matrix products, attend(): weights = jnp.exp(logits - peak)  24.4 us
    dot_general x3, matrix products, attend(): jnp.einsum('bhqk,bkhd->bqhd', probs, v_part, preferred_element_type=jnp.f...  15.7 us
    dot_general x1, matrix products, shards(): jnp.dot(flat_states, qkv_weight, preferred_element_type=jnp.float32)  15.3 us

commit v1 on v0

v1 whole, which is shorter than its diff:
```python
import functools

import jax
import jax.numpy as jnp
from jax import lax
from jax.experimental import pallas as pl
from jax.experimental.pallas import tpu as pltpu
from jax.sharding import PartitionSpec as P

HEADS = 16
HEAD = 64
AXES = ("dp", "shard")
LANES = 128


def my_rank():
    return lax.axis_index("dp") * lax.axis_size("shard") + lax.axis_index("shard")


def coords(rank):
    shard_count = lax.axis_size("shard")
    return (rank // shard_count, rank % shard_count)


def encode_kernel(
    text_dev,
    lengths_ref,
    dealing_ref,
    hidden_ref,
    qkv_weight_ref,
    qkv_bias_ref,
    out_weight_ref,
    out_bias_ref,
    gain_ref,
    shift_ref,
    query_ref,
    qkv_ref,
    context_ref,
    rows_ref,
):
    step = pl.program_id(0)
    text_len = lengths_ref[dealing_ref[my_rank() * text_dev + step]]
    seq_len, width = hidden_ref.shape[1], hidden_ref.shape[2]
    states = hidden_ref[0]

    chunk = 512
    for start in range(0, 3 * width, chunk):
        cols = slice(start, start + chunk)
        part = (
            jnp.dot(states, qkv_weight_ref[:, cols], preferred_element_type=jnp.float32)
            + qkv_bias_ref[:, cols]
        )
        if start < width:
            part = part * (1.0 / HEAD**0.5)
        qkv_ref[:, cols] = part.astype(jnp.bfloat16)

    lane = lax.broadcasted_iota(jnp.int32, (seq_len, LANES), 1)
    first = lane < HEAD
    key_pos = lax.broadcasted_iota(jnp.int32, (1, seq_len), 1)
    key_bias = jnp.where(key_pos < text_len, 0.0, -1e30).astype(jnp.float32)
    zero = jnp.zeros((seq_len, LANES), jnp.bfloat16)
    ones = jnp.ones((seq_len, LANES), jnp.bfloat16)
    ones_a = jnp.where(first, ones, zero)
    ones_b = jnp.where(first, zero, ones)
    for pair in range(width // LANES):
        base = pair * LANES
        q2 = qkv_ref[:, base : base + LANES]
        k2 = qkv_ref[:, width + base : width + base + LANES]
        v2 = qkv_ref[:, 2 * width + base : 2 * width + base + LANES]
        probs = []
        for keys in (jnp.where(first, k2, zero), jnp.where(first, zero, k2)):
            logits = lax.dot_general(
                q2, keys, (((1,), (1,)), ((), ())), preferred_element_type=jnp.float32
            )
            logits = logits + key_bias
            peak = jnp.max(logits, axis=-1, keepdims=True)
            probs.append(jnp.exp(logits - peak).astype(jnp.bfloat16))
        both = jnp.concatenate(probs, axis=1)
        values = jnp.concatenate(
            [
                jnp.concatenate([jnp.where(first, v2, zero), ones_a], axis=1),
                jnp.concatenate([jnp.where(first, zero, v2), ones_b], axis=1),
            ],
            axis=0,
        )
        mixed = jnp.dot(both, values, preferred_element_type=jnp.float32)
        context_ref[:, base : base + LANES] = (mixed[:, :LANES] / mixed[:, LANES:]).astype(
            jnp.bfloat16
        )

    resid = (
        states.astype(jnp.float32)
        + jnp.dot(context_ref[...], out_weight_ref[...], preferred_element_type=jnp.float32)
        + out_bias_ref[...]
    )
    centre = jnp.mean(resid, axis=-1, keepdims=True)
    resid = resid - centre
    spread = jnp.mean(resid * resid, axis=-1, keepdims=True)
    row_pos = lax.broadcasted_iota(jnp.int32, (seq_len, 1), 0)
    scale = jnp.where(row_pos < text_len, lax.rsqrt(spread + 1e-05), 0.0)
    total = jnp.sum(resid * scale, axis=0, keepdims=True)
    pooled = total / text_len.astype(jnp.float32) * gain_ref[...] + shift_ref[...]
    query = pooled * lax.rsqrt(jnp.sum(pooled * pooled, axis=-1, keepdims=True) + 1e-06)

    @pl.when(step == 0)
    def _():
        rows_ref[...] = jnp.zeros_like(rows_ref)

    rows_ref[pl.ds(step, 1), :] = query

    @pl.when(step == text_dev - 1)
    def _():
        query_ref[...] = rows_ref[...].astype(jnp.bfloat16)


def greet(device_count, me):
    barrier = pltpu.get_barrier_semaphore()

    def signal(off, carry):
        pl.semaphore_signal(
            barrier,
            inc=1,
            device_id=coords(lax.rem(me + off, device_count)),
            device_id_type=pl.DeviceIdType.MESH,
        )
        return carry

    lax.fori_loop(1, device_count, signal, 0)
    pl.semaphore_wait(barrier, device_count - 1)


def gather_kernel(
    device_count, query_ref, cand_ref, queries_ref, cands_ref, send_sems, recv_sems, local_sems
):
    me = my_rank()
    greet(device_count, me)
    pairs = ((query_ref, queries_ref), (cand_ref, cands_ref))

    def remote(which, peer, source):
        src, dst = pairs[which]
        return pltpu.make_async_remote_copy(
            src_ref=src,
            dst_ref=dst.at[source],
            send_sem=send_sems.at[which, peer],
            recv_sem=recv_sems.at[which, source],
            device_id=coords(peer),
            device_id_type=pl.DeviceIdType.MESH,
        )

    def send(off, carry):
        peer = lax.rem(me + off, device_count)
        for which in range(2):
            remote(which, peer, me).start()
        return carry

    lax.fori_loop(1, device_count, send, 0)
    local = [
        pltpu.make_async_copy(src, dst.at[me], local_sems.at[which])
        for which, (src, dst) in enumerate(pairs)
    ]
    for copy in local:
        copy.start()
    for copy in local:
        copy.wait()

    def finish(off, carry):
        peer = lax.rem(me + off, device_count)
        for which in range(2):
            remote(which, peer, peer).wait_recv()
            remote(which, peer, me).wait_send()
        return carry

    lax.fori_loop(1, device_count, finish, 0)


def score_kernel(
    dealt_ref, query_ref, cand_ref, index_ref, out_ref, text_query_ref, text_dev
):
    step = pl.program_id(0)
    padded = query_ref.shape[0]
    rows_step = index_ref.shape[0]

    @pl.when(step == 0)
    def _():
        spot = lax.broadcasted_iota(jnp.int32, (padded, padded), 0)
        pick = jnp.where(dealt_ref[...] == spot, 1.0, 0.0).astype(jnp.bfloat16)
        text_query_ref[...] = jnp.dot(
            pick, query_ref[...], preferred_element_type=jnp.float32
        ).astype(jnp.bfloat16)
        out_ref[...] = jnp.zeros_like(out_ref)

    scores = lax.dot_general(
        text_query_ref[...],
        index_ref[...],
        (((1,), (1,)), ((), ())),
        preferred_element_type=jnp.float32,
    )
    local = cand_ref[...] - (my_rank() * pl.num_programs(0) + step) * rows_step
    group = local >> 7
    lane = local & (LANES - 1)
    total = out_ref[...]
    for part in range(rows_step // LANES):
        found = jnp.take_along_axis(
            scores[:, part * LANES : (part + 1) * LANES], lane, axis=1, mode="promise_in_bounds"
        )
        total = jnp.where(group == part, found, total)
    out_ref[...] = total


def exchange_kernel(device_count, terms_ref, out_ref, arrived, send_sems, recv_sems):
    me = my_rank()
    greet(device_count, me)

    def remote(peer, source):
        return pltpu.make_async_remote_copy(
            src_ref=terms_ref.at[peer],
            dst_ref=arrived.at[source],
            send_sem=send_sems.at[peer],
            recv_sem=recv_sems.at[source],
            device_id=coords(peer),
            device_id_type=pl.DeviceIdType.MESH,
        )

    def send(off, carry):
        remote(lax.rem(me + off, device_count), me).start()
        return carry

    lax.fori_loop(1, device_count, send, 0)
    arrived[me] = terms_ref[me]

    def finish(off, carry):
        peer = lax.rem(me + off, device_count)
        remote(peer, peer).wait_recv()
        remote(peer, me).wait_send()
        return carry

    lax.fori_loop(1, device_count, finish, 0)
    total = jnp.sum(arrived[...], axis=0)
    out_ref[...] = total[: out_ref.shape[0], : out_ref.shape[1]]


def shards(
    hidden,
    lengths,
    dealing,
    candidates,
    index_rows,
    qkv_weight,
    qkv_bias,
    out_weight,
    out_bias,
    norm_gain,
    norm_shift,
):
    text_dev, seq_len, width = hidden.shape
    device_count = lax.axis_size(AXES)
    cand_count = candidates.shape[1]
    slots = -(-text_dev // 8) * 8
    padded = device_count * slots
    vmem = pl.BlockSpec(memory_space=pltpu.VMEM)

    def whole(*shape):
        return pl.BlockSpec(
            shape, lambda *_: (0,) * len(shape), pipeline_mode=pl.Buffered(1)
        )

    query = pl.pallas_call(
        functools.partial(encode_kernel, text_dev),
        grid_spec=pltpu.PrefetchScalarGridSpec(
            num_scalar_prefetch=2,
            grid=(text_dev,),
            in_specs=[
                pl.BlockSpec((1, seq_len, width), lambda i, *_: (i, 0, 0)),
                whole(width, 3 * width),
                whole(1, 3 * width),
                whole(width, width),
                whole(1, width),
                whole(1, width),
                whole(1, width),
            ],
            out_specs=pl.BlockSpec((slots, width), lambda i, *_: (0, 0)),
            scratch_shapes=[
                pltpu.VMEM((seq_len, 3 * width), jnp.bfloat16),
                pltpu.VMEM((seq_len, width), jnp.bfloat16),
                pltpu.VMEM((slots, width), jnp.float32),
            ],
        ),
        out_shape=jax.ShapeDtypeStruct((slots, width), jnp.bfloat16),
        compiler_params=pltpu.CompilerParams(vmem_limit_bytes=40 << 20),
        name="encode",
    )(
        lengths,
        dealing,
        hidden,
        qkv_weight,
        qkv_bias[None, :],
        out_weight,
        out_bias[None, :],
        norm_gain[None, :],
        norm_shift[None, :],
    )

    cand_block = jnp.pad(
        candidates, ((0, slots - text_dev), (0, LANES - cand_count)), constant_values=-1
    )
    queries, cands = pl.pallas_call(
        functools.partial(gather_kernel, device_count),
        in_specs=[vmem, vmem],
        out_specs=[vmem, vmem],
        out_shape=[
            jax.ShapeDtypeStruct((device_count, slots, width), jnp.bfloat16),
            jax.ShapeDtypeStruct((device_count, slots, LANES), jnp.int32),
        ],
        scratch_shapes=[
            pltpu.SemaphoreType.DMA((2, device_count)),
            pltpu.SemaphoreType.DMA((2, device_count)),
            pltpu.SemaphoreType.DMA((2,)),
        ],
        compiler_params=pltpu.CompilerParams(collective_id=0, has_side_effects=True),
        name="gather",
    )(query, cand_block)

    dealt = dealing.reshape(device_count, text_dev)
    dealt = dealt // text_dev * slots + dealt % text_dev
    dealt = jnp.pad(dealt, ((0, 0), (0, slots - text_dev)), constant_values=-1)
    rows_step = 1024
    terms = pl.pallas_call(
        functools.partial(score_kernel, text_dev=text_dev),
        grid=(index_rows.shape[0] // rows_step,),
        in_specs=[
            whole(1, padded),
            whole(padded, width),
            whole(padded, LANES),
            pl.BlockSpec((rows_step, width), lambda i: (i, 0)),
        ],
        out_specs=pl.BlockSpec((padded, LANES), lambda i: (0, 0)),
        out_shape=jax.ShapeDtypeStruct((padded, LANES), jnp.float32),
        scratch_shapes=[pltpu.VMEM((padded, width), jnp.bfloat16)],
        compiler_params=pltpu.CompilerParams(vmem_limit_bytes=40 << 20),
        name="score",
    )(
        dealt.reshape(1, padded),
        queries.reshape(padded, width),
        cands.reshape(padded, LANES),
        index_rows,
    )

    return pl.pallas_call(
        functools.partial(exchange_kernel, device_count),
        in_specs=[vmem],
        out_specs=vmem,
        out_shape=jax.ShapeDtypeStruct((text_dev, cand_count), jnp.float32),
        scratch_shapes=[
            pltpu.VMEM((device_count, slots, LANES), jnp.float32),
            pltpu.SemaphoreType.DMA((device_count,)),
            pltpu.SemaphoreType.DMA((device_count,)),
        ],
        compiler_params=pltpu.CompilerParams(collective_id=1, has_side_effects=True),
        name="exchange",
    )(terms.reshape(device_count, slots, LANES))


def solution(mesh):
    in_specs = (
        P(("dp", "shard"), None, None),
        P(),
        P(),
        P(("dp", "shard"), None),
        P(("dp", "shard"), None),
        P(),
        P(),
        P(),
        P(),
        P(),
        P(),
    )
    out_specs = P(("dp", "shard"), None)
    return jax.shard_map(shards, mesh=mesh, in_specs=in_specs, out_specs=out_specs, check_vma=False)
```

time: 321 us -> 87.1 us (0.27)
  blocking collectives: 133 us -> 0 us
  matrix products: 70.3 us -> 0 us
  other arithmetic: 68.9 us -> 1.39 us
  Pallas kernels: 0 us -> 65.1 us
  local copies, waits for them, and re-layouts: 47.3 us -> 19.9 us
    all_gather x2 -> x0, blocking collectives: 81.6 us -> none  [the longest x1 44.6 us: shards(): segment = lax.all_gather(queries, ('dp', 'shard'), axis=0, tiled=True)]
    pallas_call x0 -> x4, Pallas kernels: none -> 65.1 us  [the longest x1 26.1 us: shards(): pl.pallas_call(functools.partial(encode_kernel, text_dev), grid_spec=pltp...]
    reduce_sum x20 -> x0, other arithmetic: 60.8 us -> none  [the longest x16 58.5 us: pick_group(): return jnp.sum(jnp.where(matches, block_scores[:, None, :], 0.0), axis=-1)]
    dot_general x6 -> x0, matrix products: 45.8 us -> none  [the longest x3 15.7 us: attend(): jnp.einsum('bhqk,bkhd->bqhd', probs, v_part, preferred_element_type=jnp.f...]
    unnamed x1 -> x0, blocking collectives: 37.9 us -> none
    dynamic_slice x6 -> x0, local copies, waits for them, and re-layouts: 25.2 us -> none  [shards(): lax.map(attend, (qkv_blocks, len_blocks))]
    sub x3 -> x0, matrix products: 24.4 us -> none  [attend(): weights = jnp.exp(logits - peak)]
    unnamed x15 -> x29, local copies, waits for them, and re-layouts: 0.38 us -> 18.2 us
where the time goes in v1:
time: 87.1 us; the launch traced here: 86.5 us
  Pallas kernels  65.1 us (75%)
  local copies, waits for them, and re-layouts  19.9 us (23%)
  other arithmetic  1.39 us (2%)
    pallas_call x1, Pallas kernels, shards(): pl.pallas_call(functools.partial(encode_kernel, text_dev), grid_spec=pltp...  26.1 us
    pallas_call x1, Pallas kernels, shards(): pl.pallas_call(functools.partial(gather_kernel, device_count), in_specs=[...  20.8 us
    unnamed x29, local copies, waits for them, and re-layouts  18.2 us
    pallas_call x1, Pallas kernels, shards(): pl.pallas_call(functools.partial(exchange_kernel, device_count), in_specs...  14 us
    pallas_call x1, Pallas kernels, shards(): pl.pallas_call(functools.partial(score_kernel, text_dev=text_dev), grid=(...  4.26 us

profile of v1, /device:TPU:0, one launch (start us, length us, event | category | flops | bytes accessed | tf_op | source)
XLA Modules:
  0.0 86.5 jit_solution(2807871281966590305)
XLA Ops:
  0.0 0.7 sign_compare_fusion
  0.7 0.7 broadcast_remainder_fusion
  1.4 0.1 ne.27
  1.5 1.3 %pad.9.cand_ref = s32[8,128]{1,0:T(8,128)} pad(s32[6,64]{1,0:T(8,128)} %param.14, s32[]{:T(128)} %constant.21.clone.1), padding=0_2x0_64 | pad | bytes 5636 | tf_op jit(solution)/shard_map/jit(_pad)/pad | solution.py:303
  2.8 0.1 rem.19
  2.9 0.1 div.10
  3.0 0.1 reshape.20.dealt_ref
  3.1 0.0 copy-start.1
  3.1 2.8 %copy-done.1 = bf16[1024,3072]{1,0:T(8,128)(2,1)S(1)} copy-done((bf16[1024,3072]{1,0:T(8,128)(2,1)S(1)}, bf16[1024,3072]{1,0:T(8,128)(2,1)}, u32[]{:S(2)}) %copy-start.1) | copy-done | bytes 6291480
  5.9 0.0 copy-start.2
  5.9 1.9 %copy-done.2 = bf16[6,256,1024]{2,1,0:T(8,128)(2,1)S(1)} copy-done((bf16[6,256,1024]{2,1,0:T(8,128)(2,1)S(1)}, bf16[6,256,1024]{2,1,0:T(8,128)(2,1)}, u32[]{:S(2)}) %copy-start.2) | copy-done | bytes 3145752
  7.8 0.0 copy-start.3
  7.8 1.6 %copy-done.3 = bf16[1024,1024]{1,0:T(8,128)(2,1)S(1)} copy-done((bf16[1024,1024]{1,0:T(8,128)(2,1)S(1)}, bf16[1024,1024]{1,0:T(8,128)(2,1)}, u32[]{:S(2)}) %copy-start.3) | copy-done | bytes 2097176
  9.4 0.0 copy-start.8
  9.4 0.7 copy-done.8
  10.1 0.0 copy-start.9
  10.1 0.7 copy-done.9
  10.8 0.0 copy-start.10
  10.8 0.7 copy-done.10
  11.5 0.0 copy-start.11
  11.5 0.7 copy-done.11
  12.1 0.0 copy-start.12
  12.2 0.7 copy-done.12
  12.8 0.0 copy-start.13
  12.8 0.7 copy-done.13
  13.5 26.1 %encode.1.query_ref = bf16[8,1024]{1,0:T(8,128)(2,1)S(1)} custom-call(s32[192]{0:T(256)S(1)} %copy-done.13, s32[192]{0:T(256)S(1)} %copy-done.12, bf16[6,256,1024]{2,1,0:T(8,128)(2,1)S(1)} %copy-done.2, bf16[1024,3072]{1,0:T(8,128)(2,1)S(1)} %copy-done.1, f32[1,3072]{1,0:T(1,128)S(1)} %bitcast.10, bf16[1024,1024]{1,0:T(8,128)(2,1)S(1)} %copy-done.3, ...), custom_call_target="tpu_custom_call" | custom-call | tf_op jit(solution)/shard_map/encode/pallas_call | solution.py:267
  39.6 0.0 copy-start.7
  39.6 0.6 copy-done.7
  40.2 20.8 %gather.1 = (bf16[32,8,1024]{2,1,0:T(8,128)(2,1)}, s32[32,8,128]{2,1,0:T(8,128)}) custom-call(bf16[8,1024]{1,0:T(8,128)(2,1)} %copy-done.7, s32[8,128]{1,0:T(8,128)} %pad.9.cand_ref), custom_call_target="tpu_custom_call" | custom-call | tf_op jit(solution)/shard_map/gather/pallas_call | solution.py:306
  61.0 0.0 copy-start
  61.0 3.4 %copy-done = bf16[4096,1024]{1,0:T(8,128)(2,1)S(1)} copy-done((bf16[4096,1024]{1,0:T(8,128)(2,1)S(1)}, bf16[4096,1024]{1,0:T(8,128)(2,1)}, u32[]{:S(2)}) %copy-start) | copy-done | bytes 8388632
  64.4 0.0 copy-start.5
  64.4 1.0 %copy-done.5 = bf16[32,8,1024]{2,1,0:T(8,128)(2,1)S(1)} copy-done((bf16[32,8,1024]{2,1,0:T(8,128)(2,1)S(1)}, bf16[32,8,1024]{2,1,0:T(8,128)(2,1)}, u32[]{:S(2)}) %copy-start.5) | copy-done | bytes 524312
  65.4 0.0 copy-start.6
  65.4 0.9 %copy-done.6 = s32[32,8,128]{2,1,0:T(8,128)S(1)} copy-done((s32[32,8,128]{2,1,0:T(8,128)S(1)}, s32[32,8,128]{2,1,0:T(8,128)}, u32[]{:S(2)}) %copy-start.6) | copy-done | bytes 131096
  66.3 4.3 %score.1 = f32[256,128]{1,0:T(8,128)S(1)} custom-call(s32[1,256]{1,0:T(1,128)S(1)} %reshape.20.dealt_ref, bf16[256,1024]{1,0:T(8,128)(2,1)S(1)} %bitcast.8, s32[256,128]{1,0:T(8,128)S(1)} %bitcast.9, bf16[4096,1024]{1,0:T(8,128)(2,1)S(1)} %copy-done), custom_call_target="tpu_custom_call" | custom-call | tf_op jit(solution)/shard_map/score/pallas_call | solution.py:327
  70.6 0.0 copy-start.4
  70.6 0.6 copy-done.4
  71.2 14.0 %exchange.1 = f32[6,64]{1,0:T(8,128)} custom-call(f32[32,8,128]{2,1,0:T(8,128)} %bitcast.7), custom_call_target="tpu_custom_call" | custom-call | tf_op jit(solution)/shard_map/exchange/pallas_call | solution.py:348
  85.2 1.3 %copy.13 = f32[6,64]{1,0:T(8,128)} copy(f32[6,64]{1,0:T(8,128)} %exchange.1) | data formatting | bytes 3072
  (2 shorter events, 0.0 us)
Async XLA Ops:
  3.1 2.8 %copy-start.1 = (bf16[1024,3072]{1,0:T(8,128)(2,1)S(1)}, bf16[1024,3072]{1,0:T(8,128)(2,1)}, u32[]{:S(2)}) copy-start(bf16[1024,3072]{1,0:T(8,128)(2,1)} %qkv_weight_ref.1) | copy-start | bytes 18874372
  5.9 1.9 %copy-start.2 = (bf16[6,256,1024]{2,1,0:T(8,128)(2,1)S(1)}, bf16[6,256,1024]{2,1,0:T(8,128)(2,1)}, u32[]{:S(2)}) copy-start(bf16[6,256,1024]{2,1,0:T(8,128)(2,1)} %hidden_ref.1) | copy-start | bytes 9437188
  7.8 1.6 %copy-start.3 = (bf16[1024,1024]{1,0:T(8,128)(2,1)S(1)}, bf16[1024,1024]{1,0:T(8,128)(2,1)}, u32[]{:S(2)}) copy-start(bf16[1024,1024]{1,0:T(8,128)(2,1)} %out_weight_ref.1) | copy-start | bytes 6291460
  9.4 0.7 copy-start.8
  10.1 0.7 copy-start.9
  10.8 0.7 copy-start.10
  11.5 0.7 copy-start.11
  12.1 0.7 copy-start.12
  12.8 0.7 copy-start.13
  39.6 0.6 copy-start.7
  61.0 3.4 %copy-start = (bf16[4096,1024]{1,0:T(8,128)(2,1)S(1)}, bf16[4096,1024]{1,0:T(8,128)(2,1)}, u32[]{:S(2)}) copy-start(bf16[4096,1024]{1,0:T(8,128)(2,1)} %index_ref.1) | copy-start | bytes 25165828
  64.4 1.0 %copy-start.5 = (bf16[32,8,1024]{2,1,0:T(8,128)(2,1)S(1)}, bf16[32,8,1024]{2,1,0:T(8,128)(2,1)}, u32[]{:S(2)}) copy-start(bf16[32,8,1024]{2,1,0:T(8,128)(2,1)} %get-tuple-element.7) | copy-start | bytes 1572868
  65.4 0.9 %copy-start.6 = (s32[32,8,128]{2,1,0:T(8,128)S(1)}, s32[32,8,128]{2,1,0:T(8,128)}, u32[]{:S(2)}) copy-start(s32[32,8,128]{2,1,0:T(8,128)} %get-tuple-element.8) | copy-start | bytes 393220
  70.6 0.7 copy-start.4

commit v2 on v0

v2 whole, which is shorter than its diff:
```python
import functools

import jax
import jax.numpy as jnp
from jax import lax
from jax.experimental import pallas as pl
from jax.experimental.pallas import tpu as pltpu
from jax.sharding import PartitionSpec as P

HEADS = 16
HEAD = 64
LANES = 128


SLOTS = 8
BATCH = 2


def encode_text(
    step, text_len, hidden_ref, weights, bias_ref, out_bias_ref, gain_ref, shift_ref, scratch
):
    qkv_weight, out_weight, qkv_wait, out_wait = weights
    qkv_ref, context_ref = scratch
    seq_len, width = hidden_ref.shape[1], hidden_ref.shape[2]
    states = hidden_ref[0]

    chunk = 512
    for start in range(0, 3 * width, chunk):
        if start % width == 0:
            pl.when(step == 0)(qkv_wait[start // width])
        cols = slice(start, start + chunk)
        part = (
            jnp.dot(states, qkv_weight[:, cols], preferred_element_type=jnp.float32)
            + bias_ref[:, cols]
        )
        if start < width:
            part = part * (1.0 / HEAD**0.5)
        qkv_ref[:, cols] = part.astype(jnp.bfloat16)

    lane = lax.broadcasted_iota(jnp.int32, (seq_len, LANES), 1)
    first = lane < HEAD
    key_pos = lax.broadcasted_iota(jnp.int32, (1, seq_len), 1)
    key_bias = jnp.where(key_pos < text_len, 0.0, -1e30).astype(jnp.float32)
    zero = jnp.zeros((seq_len, LANES), jnp.bfloat16)
    ones = jnp.ones((seq_len, LANES), jnp.bfloat16)
    ones_a = jnp.where(first, ones, zero)
    ones_b = jnp.where(first, zero, ones)
    for pair in range(width // LANES):
        base = pair * LANES
        q2 = qkv_ref[:, base : base + LANES]
        k2 = qkv_ref[:, width + base : width + base + LANES]
        v2 = qkv_ref[:, 2 * width + base : 2 * width + base + LANES]
        probs = []
        for keys in (jnp.where(first, k2, zero), jnp.where(first, zero, k2)):
            logits = lax.dot_general(
                q2, keys, (((1,), (1,)), ((), ())), preferred_element_type=jnp.float32
            )
            logits = logits + key_bias
            peak = jnp.max(logits, axis=-1, keepdims=True)
            probs.append(jnp.exp(logits - peak).astype(jnp.bfloat16))
        both = jnp.concatenate(probs, axis=1)
        values = jnp.concatenate(
            [
                jnp.concatenate([jnp.where(first, v2, zero), ones_a], axis=1),
                jnp.concatenate([jnp.where(first, zero, v2), ones_b], axis=1),
            ],
            axis=0,
        )
        mixed = jnp.dot(both, values, preferred_element_type=jnp.float32)
        context_ref[:, base : base + LANES] = (mixed[:, :LANES] / mixed[:, LANES:]).astype(
            jnp.bfloat16
        )

    pl.when(step == 0)(out_wait)
    resid = (
        states.astype(jnp.float32)
        + jnp.dot(context_ref[...], out_weight[...], preferred_element_type=jnp.float32)
        + out_bias_ref[...]
    )
    centre = jnp.mean(resid, axis=-1, keepdims=True)
    resid = resid - centre
    spread = jnp.mean(resid * resid, axis=-1, keepdims=True)
    row_pos = lax.broadcasted_iota(jnp.int32, (seq_len, 1), 0)
    scale = jnp.where(row_pos < text_len, lax.rsqrt(spread + 1e-05), 0.0)
    total = jnp.sum(resid * scale, axis=0, keepdims=True)
    pooled = total / text_len.astype(jnp.float32) * gain_ref[...] + shift_ref[...]
    return pooled * lax.rsqrt(jnp.sum(pooled * pooled, axis=-1, keepdims=True) + 1e-06)


def slot_order(entries, rows, dp_count, shard_count, text_dev):
    block, row = entries // rows, entries % rows
    place = ((block % dp_count) * shard_count + block // dp_count) * text_dev + row
    return jnp.where(row < text_dev, place, -1)


def program_kernel(
    dp_count,
    shard_count,
    text_dev,
    lengths_ref,
    dealing_ref,
    hidden_ref,
    dealt_ref,
    cand_ref,
    qkv_bias_ref,
    out_bias_ref,
    gain_ref,
    shift_ref,
    qkv_weight_hbm,
    out_weight_hbm,
    index_hbm,
    out_ref,
    qkv_weight,
    out_weight,
    index_rows,
    qkv_ref,
    context_ref,
    fold_ref,
    queries,
    cands,
    wide_queries,
    slot_queries,
    text_queries,
    pick_ref,
    terms,
    arrived,
    sums,
    arrived_dp,
    load_sems,
    dp_send,
    dp_recv,
    shard_send,
    shard_recv,
):
    step = pl.program_id(0)
    my_dp, my_shard = lax.axis_index("dp"), lax.axis_index("shard")
    me = my_dp * shard_count + my_shard
    width = hidden_ref.shape[2]
    pieces = width // LANES
    padded = dp_count * shard_count * SLOTS
    compact = dp_count * shard_count * text_dev

    def dp_peer(off):
        return lax.rem(my_dp + off, dp_count)

    def shard_peer(off):
        return lax.rem(my_shard + off, shard_count)

    def to_dp(src, dst, which, off):
        return pltpu.make_async_remote_copy(
            src_ref=src,
            dst_ref=dst,
            send_sem=dp_send.at[which, off],
            recv_sem=dp_recv.at[which, off],
            device_id=(dp_peer(off), my_shard),
            device_id_type=pl.DeviceIdType.MESH,
        )

    def to_shard(src, dst, which, off):
        return pltpu.make_async_remote_copy(
            src_ref=src,
            dst_ref=dst,
            send_sem=shard_send.at[which, off],
            recv_sem=shard_recv.at[which, off],
            device_id=(my_dp, shard_peer(off)),
            device_id_type=pl.DeviceIdType.MESH,
        )

    tail = max(text_dev - BATCH, 1)
    spans = [pl.ds(0, tail), pl.ds(tail, text_dev - tail)]

    def own(which, dp, shard):
        if which == 2:
            return cands.at[shard, dp]
        return queries.at[shard, dp, spans[which]]

    def column(which, shard):
        if which == 2:
            return cands.at[shard]
        return queries.at[shard, :, spans[which]]

    def dp_start(which):
        for off in range(1, dp_count):
            block = own(which, my_dp, my_shard)
            to_dp(block, block, which, off).start()

    def dp_finish(which):
        for off in range(1, dp_count):
            block = own(which, lax.rem(my_dp + dp_count - off, dp_count), my_shard)
            to_dp(block, block, which, off).wait_recv()
            to_dp(block, block, which, off).wait_send()

    def shard_start(which):
        for off in range(1, shard_count):
            block = column(which, my_shard)
            to_shard(block, block, which, off).start()

    def shard_finish(which):
        for off in range(1, shard_count):
            block = column(which, lax.rem(my_shard + shard_count - off, shard_count))
            to_shard(block, block, which, off).wait_recv()
            to_shard(block, block, which, off).wait_send()

    loads = [
        pltpu.make_async_copy(
            qkv_weight_hbm.at[:, pl.ds(part * width, width)],
            qkv_weight.at[:, pl.ds(part * width, width)],
            load_sems.at[part],
        )
        for part in range(3)
    ]
    loads.append(pltpu.make_async_copy(out_weight_hbm, out_weight, load_sems.at[3]))
    loads.append(pltpu.make_async_copy(index_hbm, index_rows, load_sems.at[4]))
    barrier = pltpu.get_barrier_semaphore()

    @pl.when(step == 0)
    def _():
        for load in loads:
            load.start()
        for off in range(1, dp_count):
            pl.semaphore_signal(
                barrier,
                inc=1,
                device_id=(dp_peer(off), my_shard),
                device_id_type=pl.DeviceIdType.MESH,
            )
        for off in range(1, shard_count):
            pl.semaphore_signal(
                barrier,
                inc=1,
                device_id=(my_dp, shard_peer(off)),
                device_id_type=pl.DeviceIdType.MESH,
            )
        mine = cands.at[my_shard, my_dp]
        mine[...] = jnp.full((SLOTS, LANES), -1, jnp.int32)
        mine[:text_dev, : cand_ref.shape[1]] = cand_ref[...]
        texts = slot_order(
            lax.broadcasted_iota(jnp.int32, (padded, 1), 0), SLOTS, dp_count, shard_count, text_dev
        )
        slots = slot_order(
            lax.broadcasted_iota(jnp.int32, (1, compact), 1),
            text_dev,
            dp_count,
            shard_count,
            text_dev,
        )
        holds = jnp.where(dealt_ref[...] == texts, 1.0, 0.0).astype(jnp.bfloat16)
        natural = lax.broadcasted_iota(jnp.int32, (compact, compact), 0)
        moves = jnp.where(natural == slots, 1.0, 0.0).astype(jnp.bfloat16)
        pick_ref[...] = jnp.dot(holds, moves, preferred_element_type=jnp.float32).astype(
            jnp.bfloat16
        )

    query = encode_text(
        step,
        lengths_ref[dealing_ref[me * text_dev + step]],
        hidden_ref,
        (qkv_weight, out_weight, [load.wait for load in loads[:3]], loads[3].wait),
        qkv_bias_ref,
        out_bias_ref,
        gain_ref,
        shift_ref,
        (qkv_ref, context_ref),
    )
    for piece in range(pieces):
        fold_ref[piece : piece + 1, :] = query[:, piece * LANES : (piece + 1) * LANES]
    queries[my_shard, my_dp, step] = fold_ref[...].astype(jnp.bfloat16)

    @pl.when(step == 0)
    def _():
        pl.semaphore_wait(barrier, dp_count + shard_count - 2)
        dp_start(2)

    @pl.when(step == 1)
    def _():
        dp_finish(2)
        shard_start(2)

    @pl.when(step == tail - 1)
    def _():
        dp_start(0)

    @pl.when(step == tail)
    def _():
        dp_finish(0)
        shard_start(0)

    @pl.when(step == text_dev - 1)
    def _():
        dp_start(1)
        shard_finish(2)
        shard_finish(0)
        loads[4].wait()
        dp_finish(1)
        shard_start(1)
        shard_finish(1)

        wide_queries[...] = (
            queries[...].astype(jnp.float32).reshape(compact, pieces, LANES)
        )
        for piece in range(pieces):
            slot_queries[:, piece * LANES : (piece + 1) * LANES] = wide_queries[
                :, piece, :
            ].astype(jnp.bfloat16)
        text_queries[...] = jnp.dot(
            pick_ref[...], slot_queries[...], preferred_element_type=jnp.float32
        ).astype(jnp.bfloat16)

        rows_here = index_rows.shape[0]
        local = cands[...].reshape(padded, LANES) - me * rows_here
        group = local >> 7
        lane = local & (LANES - 1)
        total = jnp.zeros((padded, LANES), jnp.float32)
        rows_step = 1024
        for block in range(rows_here // rows_step):
            scores = lax.dot_general(
                text_queries[...],
                index_rows[block * rows_step : (block + 1) * rows_step, :],
                (((1,), (1,)), ((), ())),
                preferred_element_type=jnp.float32,
            )
            for part in range(rows_step // LANES):
                found = jnp.take_along_axis(
                    scores[:, part * LANES : (part + 1) * LANES],
                    lane,
                    axis=1,
                    mode="promise_in_bounds",
                )
                total = jnp.where(group == block * (rows_step // LANES) + part, found, total)
        terms[...] = total.reshape(terms.shape)

        for off in range(1, shard_count):
            to_shard(terms.at[shard_peer(off)], arrived.at[off], 3, off).start()
        mine = terms[my_shard]
        for off in range(1, shard_count):
            to_shard(terms.at[shard_peer(off)], arrived.at[off], 3, off).wait_recv()
            mine = mine + arrived[off]
        sums[...] = mine
        for off in range(1, dp_count):
            to_dp(sums.at[dp_peer(off)], arrived_dp.at[off], 3, off).start()
        result = sums[my_dp]
        for off in range(1, dp_count):
            to_dp(sums.at[dp_peer(off)], arrived_dp.at[off], 3, off).wait_recv()
            result = result + arrived_dp[off]
        out_ref[...] = result[: out_ref.shape[0], : out_ref.shape[1]]
        for off in range(1, shard_count):
            to_shard(terms.at[shard_peer(off)], arrived.at[off], 3, off).wait_send()
        for off in range(1, dp_count):
            to_dp(sums.at[dp_peer(off)], arrived_dp.at[off], 3, off).wait_send()


def shards(
    hidden,
    lengths,
    dealing,
    candidates,
    index_rows,
    qkv_weight,
    qkv_bias,
    out_weight,
    out_bias,
    norm_gain,
    norm_shift,
):
    text_dev, seq_len, width = hidden.shape
    dp_count, shard_count = lax.axis_size("dp"), lax.axis_size("shard")
    cand_count = candidates.shape[1]
    padded = dp_count * shard_count * SLOTS
    compact = dp_count * shard_count * text_dev
    pieces = width // LANES
    hbm = pl.BlockSpec(memory_space=pl.ANY)

    def whole(*shape):
        return pl.BlockSpec(
            shape, lambda *_: (0,) * len(shape), pipeline_mode=pl.Buffered(1)
        )

    def copy_sems(peers):
        return pltpu.SemaphoreType.DMA((4, peers))

    return pl.pallas_call(
        functools.partial(program_kernel, dp_count, shard_count, text_dev),
        grid_spec=pltpu.PrefetchScalarGridSpec(
            num_scalar_prefetch=2,
            grid=(text_dev,),
            in_specs=[
                pl.BlockSpec((1, seq_len, width), lambda i, *_: (i, 0, 0)),
                whole(1, compact),
                whole(text_dev, cand_count),
                whole(1, 3 * width),
                whole(1, width),
                whole(1, width),
                whole(1, width),
                hbm,
                hbm,
                hbm,
            ],
            out_specs=pl.BlockSpec((text_dev, cand_count), lambda i, *_: (0, 0)),
            scratch_shapes=[
                pltpu.VMEM((width, 3 * width), jnp.bfloat16),
                pltpu.VMEM((width, width), jnp.bfloat16),
                pltpu.VMEM(index_rows.shape, jnp.bfloat16),
                pltpu.VMEM((seq_len, 3 * width), jnp.bfloat16),
                pltpu.VMEM((seq_len, width), jnp.bfloat16),
                pltpu.VMEM((pieces, LANES), jnp.float32),
                pltpu.VMEM((shard_count, dp_count, text_dev, pieces, LANES), jnp.bfloat16),
                pltpu.VMEM((shard_count, dp_count, SLOTS, LANES), jnp.int32),
                pltpu.VMEM((compact, pieces, LANES), jnp.float32),
                pltpu.VMEM((compact, width), jnp.bfloat16),
                pltpu.VMEM((padded, width), jnp.bfloat16),
                pltpu.VMEM((padded, compact), jnp.bfloat16),
                pltpu.VMEM((shard_count, dp_count, SLOTS, LANES), jnp.float32),
                pltpu.VMEM((shard_count, dp_count, SLOTS, LANES), jnp.float32),
                pltpu.VMEM((dp_count, SLOTS, LANES), jnp.float32),
                pltpu.VMEM((dp_count, SLOTS, LANES), jnp.float32),
                pltpu.SemaphoreType.DMA((5,)),
                copy_sems(dp_count),
                copy_sems(dp_count),
                copy_sems(shard_count),
                copy_sems(shard_count),
            ],
        ),
        out_shape=jax.ShapeDtypeStruct((text_dev, cand_count), jnp.float32),
        compiler_params=pltpu.CompilerParams(
            vmem_limit_bytes=56 << 20, collective_id=0, has_side_effects=True
        ),
        name="program",
    )(
        lengths,
        dealing,
        hidden,
        dealing[None, :],
        candidates,
        qkv_bias[None, :],
        out_bias[None, :],
        norm_gain[None, :],
        norm_shift[None, :],
        qkv_weight,
        out_weight,
        index_rows,
    )


def solution(mesh):
    in_specs = (
        P(("dp", "shard"), None, None),
        P(),
        P(),
        P(("dp", "shard"), None),
        P(("dp", "shard"), None),
        P(),
        P(),
        P(),
        P(),
        P(),
        P(),
    )
    out_specs = P(("dp", "shard"), None)
    return jax.shard_map(shards, mesh=mesh, in_specs=in_specs, out_specs=out_specs, check_vma=False)
```

time: 321 us -> 54.6 us (0.17)
  blocking collectives: 133 us -> 0 us
  matrix products: 70.3 us -> 0 us
  other arithmetic: 68.9 us -> 0 us
  Pallas kernels: 0 us -> 53.1 us
  local copies, waits for them, and re-layouts: 47.3 us -> 1.28 us
    all_gather x2 -> x0, blocking collectives: 81.6 us -> none  [the longest x1 44.6 us: shards(): segment = lax.all_gather(queries, ('dp', 'shard'), axis=0, tiled=True)]
    reduce_sum x20 -> x0, other arithmetic: 60.8 us -> none  [the longest x16 58.5 us: pick_group(): return jnp.sum(jnp.where(matches, block_scores[:, None, :], 0.0), axis=-1)]
    pallas_call x0 -> x1, Pallas kernels: none -> 53.1 us  [shards(): pl.pallas_call(functools.partial(program_kernel, dp_count, shard_count, t...]
    dot_general x6 -> x0, matrix products: 45.8 us -> none  [the longest x3 15.7 us: attend(): jnp.einsum('bhqk,bkhd->bqhd', probs, v_part, preferred_element_type=jnp.f...]
    unnamed x1 -> x0, blocking collectives: 37.9 us -> none
    dynamic_slice x6 -> x0, local copies, waits for them, and re-layouts: 25.2 us -> none  [shards(): lax.map(attend, (qkv_blocks, len_blocks))]
    sub x3 -> x0, matrix products: 24.4 us -> none  [attend(): weights = jnp.exp(logits - peak)]
    all_to_all x1 -> x0, blocking collectives: 13.1 us -> none  [shards(): lax.all_to_all(outgoing, ('dp', 'shard'), split_axis=0, concat_axis=0, ti...]
where the time goes in v2:
time: 54.6 us; the launch traced here: 54.4 us
  Pallas kernels  53.1 us (97%)
  local copies, waits for them, and re-layouts  1.28 us (2%)
    pallas_call x1, Pallas kernels, shards(): pl.pallas_call(functools.partial(program_kernel, dp_count, shard_count, t...  53.1 us
    unnamed x1, local copies, waits for them, and re-layouts  1.28 us

profile of v2, /device:TPU:0, one launch (start us, length us, event | category | flops | bytes accessed | tf_op | source)
XLA Modules:
  0.0 54.4 jit_solution(2221237882239151546)
XLA Ops:
  0.0 53.1 %program.1 = f32[6,64]{1,0:T(8,128)} custom-call(s32[192]{0:T(256)} %lengths_ref.1, s32[192]{0:T(256)} %dealing_ref.1, bf16[6,256,1024]{2,1,0:T(8,128)(2,1)} %hidden_ref.1, s32[1,192]{1,0:T(1,128)} %bitcast.9, s32[6,64]{1,0:T(8,128)} %cand_ref.1, f32[1,3072]{1,0:T(1,128)} %bitcast.5, f32[1,1024]{1,0:T(1,128)} %bitcast.6, f32[1,1024]{1,0:T(1,128)} %bitcast.7, ...), custom_call_target="tpu_custom_call" | custom-call | tf_op jit(solution)/shard_map/program/pallas_call | solution.py:381
  53.1 1.3 %copy.13 = f32[6,64]{1,0:T(8,128)} copy(f32[6,64]{1,0:T(8,128)} %program.1) | data formatting | bytes 3072

commit v3 on v2

--- a/solution.py
+++ b/solution.py
@@ -17,7 +17,7 @@
 
 
 def encode_text(
-    step, text_len, hidden_ref, weights, bias_ref, out_bias_ref, gain_ref, shift_ref, scratch
+    loading, text_len, hidden_ref, weights, bias_ref, out_bias_ref, gain_ref, shift_ref, scratch
 ):
     qkv_weight, out_weight, qkv_wait, out_wait = weights
     qkv_ref, context_ref = scratch
@@ -26,8 +26,8 @@
 
     chunk = 512
     for start in range(0, 3 * width, chunk):
-        if start % width == 0:
-            pl.when(step == 0)(qkv_wait[start // width])
+        if loading and start % width == 0:
+            qkv_wait[start // width]()
         cols = slice(start, start + chunk)
         part = (
             jnp.dot(states, qkv_weight[:, cols], preferred_element_type=jnp.float32)
@@ -71,7 +71,8 @@
             jnp.bfloat16
         )
 
-    pl.when(step == 0)(out_wait)
+    if loading:
+        out_wait()
     resid = (
         states.astype(jnp.float32)
         + jnp.dot(context_ref[...], out_weight[...], preferred_element_type=jnp.float32)
@@ -124,13 +125,15 @@
     pick_ref,
     terms,
     arrived,
-    sums,
-    arrived_dp,
     load_sems,
     dp_send,
     dp_recv,
     shard_send,
     shard_recv,
+    all_send,
+    all_recv,
+    out_send,
+    out_recv,
 ):
     step = pl.program_id(0)
     my_dp, my_shard = lax.axis_index("dp"), lax.axis_index("shard")
@@ -188,7 +191,14 @@
         for off in range(1, dp_count):
             block = own(which, lax.rem(my_dp + dp_count - off, dp_count), my_shard)
             to_dp(block, block, which, off).wait_recv()
+
+    def sent(which):
+        for off in range(1, dp_count):
+            block = own(which, my_dp, my_shard)
             to_dp(block, block, which, off).wait_send()
+        for off in range(1, shard_count):
+            block = column(which, my_shard)
+            to_shard(block, block, which, off).wait_send()
 
     def shard_start(which):
         for off in range(1, shard_count):
@@ -199,7 +209,39 @@
         for off in range(1, shard_count):
             block = column(which, lax.rem(my_shard + shard_count - off, shard_count))
             to_shard(block, block, which, off).wait_recv()
-            to_shard(block, block, which, off).wait_send()
+
+    others = [(far, off) for far in range(1, dp_count) for off in range(1, shard_count)]
+    everyone = others + [(far, 0) for far in range(1, dp_count)]
+    everyone += [(0, off) for off in range(1, shard_count)]
+
+    def to_all(src, dst, far, off):
+        return pltpu.make_async_remote_copy(
+            src_ref=src,
+            dst_ref=dst,
+            send_sem=all_send.at[far, off],
+            recv_sem=all_recv.at[far, off],
+            device_id=(dp_peer(far), shard_peer(off)),
+            device_id_type=pl.DeviceIdType.MESH,
+        )
+
+    def all_start():
+        block = own(1, my_dp, my_shard)
+        for far, off in everyone:
+            to_all(block, block, far, off).start()
+
+    def all_finish():
+        for far, off in everyone:
+            block = own(
+                1,
+                lax.rem(my_dp + dp_count - far, dp_count),
+                lax.rem(my_shard + shard_count - off, shard_count),
+            )
+            to_all(block, block, far, off).wait_recv()
+
+    def all_sent():
+        block = own(1, my_dp, my_shard)
+        for far, off in everyone:
+            to_all(block, block, far, off).wait_send()
 
     loads = [
         pltpu.make_async_copy(
@@ -215,7 +257,7 @@
 
     @pl.when(step == 0)
     def _():
-        for load in loads:
+        for load in loads[:4]:
             load.start()
         for off in range(1, dp_count):
             pl.semaphore_signal(
@@ -231,6 +273,13 @@
                 device_id=(my_dp, shard_peer(off)),
                 device_id_type=pl.DeviceIdType.MESH,
             )
+        for far, off in others:
+            pl.semaphore_signal(
+                barrier,
+                inc=1,
+                device_id=(dp_peer(far), shard_peer(off)),
+                device_id_type=pl.DeviceIdType.MESH,
+            )
         mine = cands.at[my_shard, my_dp]
         mine[...] = jnp.full((SLOTS, LANES), -1, jnp.int32)
         mine[:text_dev, : cand_ref.shape[1]] = cand_ref[...]
@@ -251,28 +300,33 @@
             jnp.bfloat16
         )
 
-    query = encode_text(
-        step,
-        lengths_ref[dealing_ref[me * text_dev + step]],
-        hidden_ref,
-        (qkv_weight, out_weight, [load.wait for load in loads[:3]], loads[3].wait),
-        qkv_bias_ref,
-        out_bias_ref,
-        gain_ref,
-        shift_ref,
-        (qkv_ref, context_ref),
-    )
-    for piece in range(pieces):
-        fold_ref[piece : piece + 1, :] = query[:, piece * LANES : (piece + 1) * LANES]
-    queries[my_shard, my_dp, step] = fold_ref[...].astype(jnp.bfloat16)
+    def encode(loading):
+        query = encode_text(
+            loading,
+            lengths_ref[dealing_ref[me * text_dev + step]],
+            hidden_ref,
+            (qkv_weight, out_weight, [load.wait for load in loads[:3]], loads[3].wait),
+            qkv_bias_ref,
+            out_bias_ref,
+            gain_ref,
+            shift_ref,
+            (qkv_ref, context_ref),
+        )
+        for piece in range(pieces):
+            fold_ref[piece : piece + 1, :] = query[:, piece * LANES : (piece + 1) * LANES]
+        queries[my_shard, my_dp, step] = fold_ref[...].astype(jnp.bfloat16)
+
+    pl.when(step == 0)(functools.partial(encode, True))
+    pl.when(step > 0)(functools.partial(encode, False))
 
     @pl.when(step == 0)
     def _():
-        pl.semaphore_wait(barrier, dp_count + shard_count - 2)
+        pl.semaphore_wait(barrier, dp_count * shard_count - 1)
         dp_start(2)
 
     @pl.when(step == 1)
     def _():
+        loads[4].start()
         dp_finish(2)
         shard_start(2)
 
@@ -287,13 +341,11 @@
 
     @pl.when(step == text_dev - 1)
     def _():
-        dp_start(1)
+        all_start()
         shard_finish(2)
         shard_finish(0)
         loads[4].wait()
-        dp_finish(1)
-        shard_start(1)
-        shard_finish(1)
+        all_finish()
 
         wide_queries[...] = (
             queries[...].astype(jnp.float32).reshape(compact, pieces, LANES)
@@ -329,24 +381,29 @@
                 total = jnp.where(group == block * (rows_step // LANES) + part, found, total)
         terms[...] = total.reshape(terms.shape)
 
-        for off in range(1, shard_count):
-            to_shard(terms.at[shard_peer(off)], arrived.at[off], 3, off).start()
-        mine = terms[my_shard]
-        for off in range(1, shard_count):
-            to_shard(terms.at[shard_peer(off)], arrived.at[off], 3, off).wait_recv()
-            mine = mine + arrived[off]
-        sums[...] = mine
-        for off in range(1, dp_count):
-            to_dp(sums.at[dp_peer(off)], arrived_dp.at[off], 3, off).start()
-        result = sums[my_dp]
-        for off in range(1, dp_count):
-            to_dp(sums.at[dp_peer(off)], arrived_dp.at[off], 3, off).wait_recv()
-            result = result + arrived_dp[off]
+        def deliver(far, off):
+            return pltpu.make_async_remote_copy(
+                src_ref=terms.at[shard_peer(off), dp_peer(far)],
+                dst_ref=arrived.at[off, far],
+                send_sem=out_send.at[far, off],
+                recv_sem=out_recv.at[far, off],
+                device_id=(dp_peer(far), shard_peer(off)),
+                device_id_type=pl.DeviceIdType.MESH,
+            )
+
+        for far, off in everyone:
+            deliver(far, off).start()
+        for which in (0, 2):
+            sent(which)
+        all_sent()
+        result = terms[my_shard, my_dp]
+        for far, off in everyone:
+            deliver(far, off).wait_recv()
+        for far, off in everyone:
+            result = result + arrived[off, far]
         out_ref[...] = result[: out_ref.shape[0], : out_ref.shape[1]]
-        for off in range(1, shard_count):
-            to_shard(terms.at[shard_peer(off)], arrived.at[off], 3, off).wait_send()
-        for off in range(1, dp_count):
-            to_dp(sums.at[dp_peer(off)], arrived_dp.at[off], 3, off).wait_send()
+        for far, off in everyone:
+            deliver(far, off).wait_send()
 
 
 def shards(
@@ -411,13 +468,12 @@
                 pltpu.VMEM((padded, compact), jnp.bfloat16),
                 pltpu.VMEM((shard_count, dp_count, SLOTS, LANES), jnp.float32),
                 pltpu.VMEM((shard_count, dp_count, SLOTS, LANES), jnp.float32),
-                pltpu.VMEM((dp_count, SLOTS, LANES), jnp.float32),
-                pltpu.VMEM((dp_count, SLOTS, LANES), jnp.float32),
                 pltpu.SemaphoreType.DMA((5,)),
                 copy_sems(dp_count),
                 copy_sems(dp_count),
                 copy_sems(shard_count),
                 copy_sems(shard_count),
+                *[pltpu.SemaphoreType.DMA((dp_count, shard_count))] * 4,
             ],
         ),
         out_shape=jax.ShapeDtypeStruct((text_dev, cand_count), jnp.float32),

time: 54.6 us -> 51.2 us (0.938)
  Pallas kernels: 53.1 us -> 49.7 us
    pallas_call x1, Pallas kernels: 53.1 us -> 49.7 us  [shards(): pl.pallas_call(functools.partial(program_kernel, dp_count, shard_count, t...]
where the time goes in v3:
time: 51.2 us; the launch traced here: 51 us
  Pallas kernels  49.7 us (97%)
  local copies, waits for them, and re-layouts  1.28 us (2%)
    pallas_call x1, Pallas kernels, shards(): pl.pallas_call(functools.partial(program_kernel, dp_count, shard_count, t...  49.7 us
    unnamed x1, local copies, waits for them, and re-layouts  1.28 us

profile of v3, /device:TPU:0, one launch (start us, length us, event | category | flops | bytes accessed | tf_op | source)
XLA Modules:
  0.0 51.0 jit_solution(14572999889952194606)
XLA Ops:
  0.0 49.7 %program.1 = f32[6,64]{1,0:T(8,128)} custom-call(s32[192]{0:T(256)} %lengths_ref.1, s32[192]{0:T(256)} %dealing_ref.1, bf16[6,256,1024]{2,1,0:T(8,128)(2,1)} %hidden_ref.1, s32[1,192]{1,0:T(1,128)} %bitcast.9, s32[6,64]{1,0:T(8,128)} %cand_ref.1, f32[1,3072]{1,0:T(1,128)} %bitcast.5, f32[1,1024]{1,0:T(1,128)} %bitcast.6, f32[1,1024]{1,0:T(1,128)} %bitcast.7, ...), custom_call_target="tpu_custom_call" | custom-call | tf_op jit(solution)/shard_map/program/pallas_call | solution.py:438
  49.7 1.3 %copy.13 = f32[6,64]{1,0:T(8,128)} copy(f32[6,64]{1,0:T(8,128)} %program.1) | data formatting | bytes 3072
